TPU v7x, 32 devices: a whole 2x2x4 slice. The times are simulated.
32 devices in a mesh: row: 8 (over y, x, core), col: 4 (over z).
Axes of the slice: x: 2, y: 2, z: 4, core: 2. Of those that a mesh axis runs over, the one named last changes fastest.
Arguments:
- features: bfloat16 [512, 128, 128], P('row', 'col'), may hold values from -6 to 6
- cotangent: bfloat16 [512, 128, 128], P('row', 'col'), may hold values from -6 to 6
- kernels: bfloat16 [2, 9, 128, 128], replicated, may hold values from -0.1875 to 0.1875
- momentum: float32 [2, 147456], replicated, may hold values from -6 to 6
- mlp_in_weight: float32 [32, 3], replicated, may hold values from -3.5 to 3.5
- mlp_in_bias: float32 [32], replicated, may hold values from -3 to 3
- mlp_out_weight: float32 [2, 32], replicated, may hold values from -1 to 1
- mlp_out_bias: float32 [2], replicated, may hold values from -3 to 3
Outputs:
- update: float32 [2, 147456], replicated
- momentum_out: float32 [2, 147456], replicated
All inputs are finite; a program needn't handle non-finite values.
Results may differ from a plain program's by a relative error of at most 0.0014.
Values may be sent and summed in bfloat16 or wider, within the bound.
A program may use at most 64 MiB of HBM per device.

v0:
```python
import math
import jax
import jax.numpy as jnp
from jax import lax
from jax.sharding import PartitionSpec as P


def padded_2(cells, sides, width):
    for axis, dim in sides:
        count = lax.axis_size(axis)
        head = lax.slice_in_dim(cells, 0, width, axis=dim)
        tail = lax.slice_in_dim(cells, cells.shape[dim] - width, cells.shape[dim], axis=dim)
        cells = jnp.concatenate(
            [
                lax.ppermute(tail, axis, [(i, (i + 1) % count) for i in range(count)]),
                cells,
                lax.ppermute(head, axis, [((i + 1) % count, i) for i in range(count)]),
            ],
            axis=dim,
        )
    return cells


def convolve(padded, kernel, tile_rows, tile_cols):
    channels = padded.shape[-1]
    summed = jnp.zeros((tile_rows * tile_cols, kernel.shape[-1]), jnp.float32)
    for tap_row in range(3):
        for tap_col in range(3):
            window = padded[tap_row : tap_row + tile_rows, tap_col : tap_col + tile_cols].reshape(
                tile_rows * tile_cols, channels
            )
            summed = summed + jnp.dot(
                window, kernel[3 * tap_row + tap_col], preferred_element_type=jnp.float32
            )
    return summed.reshape(tile_rows, tile_cols, -1)


def kernel_grad(padded, cotangent, tile_rows, tile_cols):
    channels = padded.shape[-1]
    flat_cot = cotangent.reshape(tile_rows * tile_cols, -1)
    taps = []
    for tap_row in range(3):
        for tap_col in range(3):
            window = padded[tap_row : tap_row + tile_rows, tap_col : tap_col + tile_cols].reshape(
                tile_rows * tile_cols, channels
            )
            taps.append(
                lax.dot_general(
                    window, flat_cot, (((0,), (0,)), ((), ())), preferred_element_type=jnp.float32
                )
            )
    return jnp.stack(taps)


def transpose_conv(cot_pad, kernel, tile_rows, tile_cols):
    channels = cot_pad.shape[-1]
    summed = jnp.zeros((tile_rows * tile_cols, kernel.shape[-2]), jnp.float32)
    for tap_row in range(3):
        for tap_col in range(3):
            window = cot_pad[
                2 - tap_row : 2 - tap_row + tile_rows, 2 - tap_col : 2 - tap_col + tile_cols
            ].reshape(tile_rows * tile_cols, channels)
            summed = summed + lax.dot_general(
                window,
                kernel[3 * tap_row + tap_col],
                (((1,), (1,)), ((), ())),
                preferred_element_type=jnp.float32,
            )
    return summed.reshape(tile_rows, tile_cols, -1)


def learned_step(grads, squares, momentum, weights, w_in, b_in, w_out, b_out, gain, count):
    norm_scale = 1.0 / jnp.sqrt(squares / count + 1e-06)
    g_hat = grads * norm_scale[:, None]
    momentum_new = 0.9 * momentum + 0.1 * g_hat
    scaled = weights.astype(jnp.float32) * gain
    pre_units = (
        w_in[:, 0][:, None, None] * g_hat[None] + w_in[:, 1][:, None, None] * momentum_new[None]
    )
    pre_units = pre_units + w_in[:, 2][:, None, None] * scaled[None] + b_in[:, None, None]
    units = jax.nn.silu(pre_units)
    mlp_result = (
        jnp.einsum("kh,hlp->klp", w_out, units, precision=lax.Precision.HIGHEST)
        + b_out[:, None, None]
    )
    update = mlp_result[0] * jnp.exp(jnp.tanh(mlp_result[1]))
    return (update, momentum_new)


def on_device(
    features, cotangent, kernels, momentum, mlp_in_weight, mlp_in_bias, mlp_out_weight, mlp_out_bias
):
    tile_rows, tile_cols, channels = features.shape
    param_count = 9 * channels * channels
    image_pad = padded_2(features, (("row", 0), ("col", 1)), 1)
    pre_act = convolve(image_pad, kernels[0], tile_rows, tile_cols)
    hidden = jax.nn.silu(pre_act).astype(jnp.bfloat16)
    hidden_pad = padded_2(hidden, (("row", 0), ("col", 1)), 1)
    cot_pad = padded_2(cotangent, (("row", 0), ("col", 1)), 1)
    grad_two = kernel_grad(hidden_pad, cotangent, tile_rows, tile_cols)
    back_grad = transpose_conv(cot_pad, kernels[1], tile_rows, tile_cols)
    sigma_val = jax.nn.sigmoid(pre_act)
    pre_grad = (back_grad * sigma_val * (1.0 + pre_act * (1.0 - sigma_val))).astype(jnp.bfloat16)
    grad_one = kernel_grad(image_pad, pre_grad, tile_rows, tile_cols)
    local_grads = jnp.stack([grad_one.reshape(-1), grad_two.reshape(-1)])
    weights = kernels.reshape(2, param_count)
    gain = math.sqrt(9.0 * channels)
    grads = lax.psum(local_grads, ("row", "col"))
    squares = jnp.sum(grads * grads, axis=1)
    update, momentum_out = learned_step(
        grads,
        squares,
        momentum,
        weights,
        mlp_in_weight,
        mlp_in_bias,
        mlp_out_weight,
        mlp_out_bias,
        gain,
        float(param_count),
    )
    return (update, momentum_out)


def solution(mesh):
    placed = (P("row", "col", None), P("row", "col", None), P(), P(), P(), P(), P(), P())
    return jax.shard_map(
        on_device, mesh=mesh, in_specs=placed, out_specs=(P(), P()), check_vma=False
    )
```

profile of v0, /device:TPU:0, one launch (start us, length us, event | category | flops | bytes accessed | tf_op | source)
XLA Modules:
  0.0 238.4 jit_solution(3576847353787842551)
XLA Ops:
  7.2 1.3 copy.30
  8.6 0.5 collective-permute-start
  9.1 2.9 %collective-permute-start.1 = (bf16[1,32,128]{2,0,1:T(2,128)(2,1)S(1)}, bf16[1,32,128]{2,0,1:T(2,128)(2,1)S(1)}, u32[]{:S(2)}, u32[]{:S(2)}) collective-permute-start(bf16[1,32,128]{2,0,1:T(2,128)(2,1)S(1)} %get-tuple-element.41), channel_id=1, source_target_pairs={{4,0},{8,4},{12,8},{16,12},{20,16},{24,20},{28,24},{0,28},{5,1},{9... | collective-permute-start | bytes 24584 | tf_op jit(solution)/shard_map/ppermute | solution.py:17
  12.1 0.7 fusion.119
  12.8 2.6 %collective-permute-start.4 = (bf16[1,32,128]{2,1,0:T(8,128)(2,1)S(1)}, bf16[1,32,128]{2,1,0:T(8,128)(2,1)S(1)}, u32[]{:S(2)}, u32[]{:S(2)}) collective-permute-start(bf16[1,32,128]{2,1,0:T(8,128)(2,1)S(1)} %get-tuple-element.34), channel_id=1, source_target_pairs={{4,0},{8,4},{12,8},{16,12},{20,16},{24,20},{28,24},{0,28},{5,1},{9... | collective-permute-start | bytes 24584 | tf_op jit(solution)/shard_map/ppermute | solution.py:17
  15.5 2.3 collective-permute-start.2
  17.8 2.1 collective-permute-start.7
  20.8 0.4 pad_maximum_fusion.7
  21.2 0.3 copy.35
  21.5 0.3 copy.41
  21.9 2.0 collective-permute-start.5
  23.9 0.5 collective-permute-start.6
  24.4 0.3 pad_maximum_fusion.1
  24.8 0.6 fusion.116
  25.4 0.3 copy.33
  26.0 0.3 copy.36
  26.4 0.3 copy.37
  27.8 2.3 collective-permute-done.6
  30.1 0.7 pad_maximum_fusion.11
  32.0 0.7 copy-done.4
  35.7 0.4 fusion.21
  36.0 1.4 fusion.43
  38.5 0.3 fusion.38
  38.8 0.4 fusion.37
  39.2 0.3 fusion.36
  39.6 0.3 fusion.35
  40.1 2.6 %collective-permute-start.9 = (bf16[1,32,128]{2,0,1:T(2,128)(2,1)S(1)}, bf16[1,32,128]{2,0,1:T(2,128)(2,1)S(1)}, u32[]{:S(2)}, u32[]{:S(2)}) collective-permute-start(bf16[1,32,128]{2,0,1:T(2,128)(2,1)S(1)} %get-tuple-element.37), channel_id=1, source_target_pairs={{4,0},{8,4},{12,8},{16,12},{20,16},{24,20},{28,24},{0,28},{5,1},{9... | collective-permute-start | bytes 24584 | tf_op jit(solution)/shard_map/ppermute | solution.py:17
  43.0 1.2 collective-permute-done.8
  44.3 4.0 %collective-permute-start.11 = (bf16[66,1,128]{2,0,1:T(8,128)(2,1)S(1)}, bf16[66,1,128]{2,0,1:T(8,128)(2,1)S(1)}, u32[]{:S(2)}, u32[]{:S(2)}) collective-permute-start(bf16[66,1,128]{2,0,1:T(8,128)(2,1)S(1)} %get-tuple-element.20), channel_id=1, source_target_pairs={{1,0},{2,1},{3,2},{0,3},{5,4},{6,5},{7,6},{4,7},{9,8},{10,9},{11,1... | collective-permute-start | bytes 50696 | tf_op jit(solution)/shard_map/ppermute | solution.py:17
  48.6 1.2 collective-permute-done.10
  49.8 0.4 pad_maximum_fusion.2
  50.2 0.4 fusion.32
  50.6 0.5 fusion.31
  51.1 0.4 fusion.30
  51.4 0.4 fusion.29
  51.9 0.4 fusion.28
  52.3 0.4 fusion.27
  52.7 0.4 fusion.26
  53.2 0.5 fusion.25
  53.7 0.4 fusion.24
  54.1 1.9 pad_maximum_fusion
  56.2 4.3 %copy.91 = f32[1,2,1152,128]{3,1,2,0:T(2,128)S(1)} copy(f32[1,2,1152,128]{3,2,1,0:T(8,128)S(1)} %bitcast.218) | data formatting | bytes 2359296
  60.5 127.9 %all-reduce.2.cloned.1.call-done = f32[2,147456]{1,0:T(2,128)} async-done(((f32[2,147456]{1,0:T(2,128)}), f32[2,147456]{1,0:T(2,128)}) %all-reduce.2.cloned.1.call-update) | async-done | bytes 1179664 | tf_op jit(solution)/shard_map/psum | solution.py:108
  188.4 2.5 %multiply_reduce_fusion = f32[2]{0:T(128)S(1)} fusion(f32[2,147456]{1,0:T(2,128)} %all-reduce.2.cloned.1.call-done), kind=kLoop, calls=%fused_computation.45 | loop fusion | flops 589822 | bytes 1179656 | tf_op jit(solution)/shard_map/reduce_sum | solution.py:109
  191.0 1.3 multiply_add_fusion
  192.4 33.7 %fusion = f32[2,2,147456]{2,0,1:T(2,128)S(1)} fusion(f32[32]{0:T(128)S(1)} %copy-done.8, f32[2,147456]{1,0:T(2,128)S(1)} %bitcast.239, f32[32]{0:T(128)S(1)} %get-tuple-element.43, f32[2,147456]{1,0:T(2,128)S(1)} %get-tuple-element.2, f32[32]{0:T(128)S(1)} %get-tuple-element.44, f32[2,147456]{1,0:T(2,128)S(1)} %get-tuple-element.3, ...), kind=kOutput, calls=%fused_computation.1 | convolution fusion | flops 321454080 | bytes 5899016 | tf_op jit(solution)/shard_map/kh,hlp->klp/dot_general | solution.py:83
  226.1 2.5 %fusion.23 = f32[1,2,147456]{2,0,1:T(1,128)S(1)} fusion(f32[2,2,147456]{2,0,1:T(2,128)S(1)} %fusion), kind=kLoop, calls=%fused_computation.40 | loop fusion | flops 294912 | bytes 3538944 | tf_op jit(solution)/shard_map/mul | solution.py:86
  228.6 2.7 %copy.92 = f32[1,2,147456]{2,1,0:T(2,128)} copy(f32[1,2,147456]{2,0,1:T(1,128)S(1)} %fusion.23) | data formatting | bytes 2359296
  (69 shorter events, 8.4 us)
Async XLA Ops:
  7.2 185.2 %copy-start = (f32[2,32]{1,0:T(2,128)S(1)}, f32[2,32]{1,0:T(2,128)}, u32[]{:S(2)}) copy-start(f32[2,32]{1,0:T(2,128)} %param.14) | copy-start | bytes 772
  7.2 12.7 %copy-start.3 = (bf16[64,32,128]{2,1,0:T(8,128)(2,1)S(1)}, bf16[64,32,128]{2,1,0:T(8,128)(2,1)}, u32[]{:S(2)}) copy-start(bf16[64,32,128]{2,1,0:T(8,128)(2,1)} %param.9) | copy-start | bytes 1572868
  7.2 181.2 %all-reduce.2.cloned.1.call-start = ((), (), s32[]{:S(2)}) async-start(), calls=%async_computation | async-start | bytes 2359296 | tf_op jit(solution)/shard_map/psum | solution.py:108
  8.6 6.8 %collective-permute-start = (bf16[1,32,128]{2,0,1:T(2,128)(2,1)S(1)}, bf16[1,32,128]{2,0,1:T(2,128)(2,1)S(1)}, u32[]{:S(2)}, u32[]{:S(2)}) collective-permute-start(bf16[1,32,128]{2,0,1:T(2,128)(2,1)S(1)} %get-tuple-element.40), channel_id=1, source_target_pairs={{0,4},{4,8},{8,12},{12,16},{16,20},{20,24},{24,28},{28,0},{1,5},{5... | collective-permute-start | bytes 24584 | tf_op jit(solution)/shard_map/ppermute | solution.py:15
  9.1 6.3 %collective-permute-start.1 = (bf16[1,32,128]{2,0,1:T(2,128)(2,1)S(1)}, bf16[1,32,128]{2,0,1:T(2,128)(2,1)S(1)}, u32[]{:S(2)}, u32[]{:S(2)}) collective-permute-start(bf16[1,32,128]{2,0,1:T(2,128)(2,1)S(1)} %get-tuple-element.41), channel_id=1, source_target_pairs={{4,0},{8,4},{12,8},{16,12},{20,16},{24,20},{28,24},{0,28},{5,1},{9... | collective-permute-start | bytes 24584 | tf_op jit(solution)/shard_map/ppermute | solution.py:17
  12.8 7.1 %collective-permute-start.3 = (bf16[1,32,128]{2,1,0:T(8,128)(2,1)S(1)}, bf16[1,32,128]{2,1,0:T(8,128)(2,1)S(1)}, u32[]{:S(2)}, u32[]{:S(2)}) collective-permute-start(bf16[1,32,128]{2,1,0:T(8,128)(2,1)S(1)} %get-tuple-element.35), channel_id=1, source_target_pairs={{0,4},{4,8},{8,12},{12,16},{16,20},{20,24},{24,28},{28,0},{1,5},{5... | collective-permute-start | bytes 24584 | tf_op jit(solution)/shard_map/ppermute | solution.py:15
  12.8 7.1 %collective-permute-start.4 = (bf16[1,32,128]{2,1,0:T(8,128)(2,1)S(1)}, bf16[1,32,128]{2,1,0:T(8,128)(2,1)S(1)}, u32[]{:S(2)}, u32[]{:S(2)}) collective-permute-start(bf16[1,32,128]{2,1,0:T(8,128)(2,1)S(1)} %get-tuple-element.34), channel_id=1, source_target_pairs={{4,0},{8,4},{12,8},{16,12},{20,16},{24,20},{28,24},{0,28},{5,1},{9... | collective-permute-start | bytes 24584 | tf_op jit(solution)/shard_map/ppermute | solution.py:17
  15.4 4.8 %copy-start.2 = (bf16[2,9,128,128]{3,2,1,0:T(8,128)(2,1)S(1)}, bf16[2,9,128,128]{3,2,1,0:T(8,128)(2,1)}, u32[]{:S(2)}) copy-start(bf16[2,9,128,128]{3,2,1,0:T(8,128)(2,1)} %param.10) | copy-start | bytes 1769476
  15.5 9.0 %collective-permute-start.2 = (bf16[66,1,128]{2,0,1:T(8,128)(2,1)S(1)}, bf16[66,1,128]{2,0,1:T(8,128)(2,1)S(1)}, u32[]{:S(2)}, u32[]{:S(2)}) collective-permute-start(bf16[66,1,128]{2,0,1:T(8,128)(2,1)S(1)} %get-tuple-element.25), channel_id=1, source_target_pairs={{0,1},{1,2},{2,3},{3,0},{4,5},{5,6},{6,7},{7,4},{8,9},{9,10},{10,1... | collective-permute-start | bytes 50696 | tf_op jit(solution)/shard_map/ppermute | solution.py:15
  17.8 6.6 %collective-permute-start.7 = (bf16[66,1,128]{2,0,1:T(8,128)(2,1)S(1)}, bf16[66,1,128]{2,0,1:T(8,128)(2,1)S(1)}, u32[]{:S(2)}, u32[]{:S(2)}) collective-permute-start(bf16[66,1,128]{2,0,1:T(8,128)(2,1)S(1)} %get-tuple-element.24), channel_id=1, source_target_pairs={{1,0},{2,1},{3,2},{0,3},{5,4},{6,5},{7,6},{4,7},{9,8},{10,9},{11,1... | collective-permute-start | bytes 50696 | tf_op jit(solution)/shard_map/ppermute | solution.py:17
  21.9 5.9 %collective-permute-start.5 = (bf16[66,1,128]{2,1,0:T(2,128)(2,1)S(1)}, bf16[66,1,128]{2,1,0:T(2,128)(2,1)S(1)}, u32[]{:S(2)}, u32[]{:S(2)}) collective-permute-start(bf16[66,1,128]{2,1,0:T(2,128)(2,1)S(1)} %get-tuple-element.29), channel_id=1, source_target_pairs={{1,0},{2,1},{3,2},{0,3},{5,4},{6,5},{7,6},{4,7},{9,8},{10,9},{11,1... | collective-permute-start | bytes 50696 | tf_op jit(solution)/shard_map/ppermute | solution.py:17
  23.9 6.2 %collective-permute-start.6 = (bf16[66,1,128]{2,1,0:T(2,128)(2,1)S(1)}, bf16[66,1,128]{2,1,0:T(2,128)(2,1)S(1)}, u32[]{:S(2)}, u32[]{:S(2)}) collective-permute-start(bf16[66,1,128]{2,1,0:T(2,128)(2,1)S(1)} %get-tuple-element.30), channel_id=1, source_target_pairs={{0,1},{1,2},{2,3},{3,0},{4,5},{5,6},{6,7},{7,4},{8,9},{9,10},{10,1... | collective-permute-start | bytes 50696 | tf_op jit(solution)/shard_map/ppermute | solution.py:15
  31.7 1.0 copy-start.4
  40.0 4.2 %collective-permute-start.8 = (bf16[1,32,128]{2,0,1:T(2,128)(2,1)S(1)}, bf16[1,32,128]{2,0,1:T(2,128)(2,1)S(1)}, u32[]{:S(2)}, u32[]{:S(2)}) collective-permute-start(bf16[1,32,128]{2,0,1:T(2,128)(2,1)S(1)} %get-tuple-element.36), channel_id=1, source_target_pairs={{0,4},{4,8},{8,12},{12,16},{16,20},{20,24},{24,28},{28,0},{1,5},{5... | collective-permute-start | bytes 24584 | tf_op jit(solution)/shard_map/ppermute | solution.py:15
  40.1 4.1 %collective-permute-start.9 = (bf16[1,32,128]{2,0,1:T(2,128)(2,1)S(1)}, bf16[1,32,128]{2,0,1:T(2,128)(2,1)S(1)}, u32[]{:S(2)}, u32[]{:S(2)}) collective-permute-start(bf16[1,32,128]{2,0,1:T(2,128)(2,1)S(1)} %get-tuple-element.37), channel_id=1, source_target_pairs={{4,0},{8,4},{12,8},{16,12},{20,16},{24,20},{28,24},{0,28},{5,1},{9... | collective-permute-start | bytes 24584 | tf_op jit(solution)/shard_map/ppermute | solution.py:17
  44.2 5.6 %collective-permute-start.10 = (bf16[66,1,128]{2,0,1:T(8,128)(2,1)S(1)}, bf16[66,1,128]{2,0,1:T(8,128)(2,1)S(1)}, u32[]{:S(2)}, u32[]{:S(2)}) collective-permute-start(bf16[66,1,128]{2,0,1:T(8,128)(2,1)S(1)} %get-tuple-element.21), channel_id=1, source_target_pairs={{0,1},{1,2},{2,3},{3,0},{4,5},{5,6},{6,7},{7,4},{8,9},{9,10},{10,1... | collective-permute-start | bytes 50696 | tf_op jit(solution)/shard_map/ppermute | solution.py:15
  44.3 5.5 %collective-permute-start.11 = (bf16[66,1,128]{2,0,1:T(8,128)(2,1)S(1)}, bf16[66,1,128]{2,0,1:T(8,128)(2,1)S(1)}, u32[]{:S(2)}, u32[]{:S(2)}) collective-permute-start(bf16[66,1,128]{2,0,1:T(8,128)(2,1)S(1)} %get-tuple-element.20), channel_id=1, source_target_pairs={{1,0},{2,1},{3,2},{0,3},{5,4},{6,5},{7,6},{4,7},{9,8},{10,9},{11,1... | collective-permute-start | bytes 50696 | tf_op jit(solution)/shard_map/ppermute | solution.py:17
  56.2 4.3 %copy-start.7 = (f32[32,3]{0,1:T(4,128)S(1)}, f32[32,3]{0,1:T(4,128)}, u32[]{:S(2)}) copy-start(f32[32,3]{0,1:T(4,128)} %param.12) | copy-start | bytes 1156
  56.2 134.7 %copy-start.5 = (f32[2,147456]{1,0:T(2,128)S(1)}, f32[2,147456]{1,0:T(2,128)}, u32[]{:S(2)}) copy-start(f32[2,147456]{1,0:T(2,128)} %param.11) | copy-start | bytes 3538948
  188.4 2.5 %copy-start.1 = (f32[2,147456]{1,0:T(2,128)S(1)}, f32[2,147456]{1,0:T(2,128)}, u32[]{:S(2)}) copy-start(f32[2,147456]{1,0:T(2,128)} %all-reduce.2.cloned.1.call-done) | copy-start | bytes 3538948
  190.9 1.4 copy-start.8
  191.0 1.4 copy-start.9
  192.3 33.8 %copy-start.6 = (f32[2,147456]{1,0:T(2,128)}, f32[2,147456]{1,0:T(2,128)S(1)}, u32[]{:S(2)}) copy-start(f32[2,147456]{1,0:T(2,128)S(1)} %get-tuple-element.2) | copy-start | bytes 3538948
Sparse Core Ops, SparseCore 0:
  56.2 132.2 all-reduce.1
where the time goes:
time: 241 us; the launch traced here: 238 us
  waiting for transfers between devices  133 us (55%)
  matrix products  46 us (19%)
  starting transfers between devices  19.8 us (8%)
  between operations  14.8 us (6%)
  local copies, waits for them, and re-layouts  13.3 us (6%)
  other arithmetic  11.9 us (5%)
    psum x1, waiting for transfers between devices, on_device(): grads = lax.psum(local_grads, ('row', 'col'))  128 us
    dot_general x1, matrix products, learned_step(): jnp.einsum('kh,hlp->klp', w_out, units, precision=lax.Precision.HIGHEST)  33.7 us
    ppermute x6, starting transfers between devices, padded_2(): lax.ppermute(head, axis, [((i + 1) % count, i) for i in range(count)])  16.3 us
    unnamed x24, local copies, waits for them, and re-layouts  9.07 us
    dot_general x18, matrix products, kernel_grad(): lax.dot_general(window, flat_cot, (((0,), (0,)), ((), ())), preferred_ele...  7.03 us
  transfers between devices with their start and end apart: 13, of which 4 were waited for; matrix products, arithmetic and copies ran while one was open for 5% of the time, Pallas kernels for 0%

commit v1 on v0

--- a/solution.py
+++ b/solution.py
@@ -105,7 +105,7 @@
     local_grads = jnp.stack([grad_one.reshape(-1), grad_two.reshape(-1)])
     weights = kernels.reshape(2, param_count)
     gain = math.sqrt(9.0 * channels)
-    grads = lax.psum(local_grads, ("row", "col"))
+    grads = lax.psum(lax.psum(local_grads, "col"), "row")
     squares = jnp.sum(grads * grads, axis=1)
     update, momentum_out = learned_step(
         grads,

time: 241 us -> 226 us (0.938)
  waiting for transfers between devices: 133 us -> 116 us
    psum x1 -> x2, waiting for transfers between devices: 128 us -> 111 us  [on_device(): grads = lax.psum(lax.psum(local_grads, 'col'), 'row')]
    unnamed x24 -> x26, local copies, waits for them, and re-layouts: 9.07 us -> 9.88 us
  transfers between devices with their start and end apart: 13 -> 14, of which waited for: 4 -> 5; matrix products, arithmetic and copies ran while one was open for 5% -> 5% of each run, Pallas kernels for 0% -> 0%
where the time goes in v1:
time: 226 us; the launch traced here: 223 us
  waiting for transfers between devices  116 us (51%)
  matrix products  46 us (20%)
  starting transfers between devices  19.8 us (9%)
  between operations  14.8 us (7%)
  local copies, waits for them, and re-layouts  14.2 us (6%)
  other arithmetic  11.9 us (5%)
    psum x2, waiting for transfers between devices, on_device(): grads = lax.psum(lax.psum(local_grads, 'col'), 'row')  111 us
    dot_general x1, matrix products, learned_step(): jnp.einsum('kh,hlp->klp', w_out, units, precision=lax.Precision.HIGHEST)  33.7 us
    ppermute x6, starting transfers between devices, padded_2(): lax.ppermute(head, axis, [((i + 1) % count, i) for i in range(count)])  16.3 us
    unnamed x26, local copies, waits for them, and re-layouts  9.88 us
    dot_general x18, matrix products, kernel_grad(): lax.dot_general(window, flat_cot, (((0,), (0,)), ((), ())), preferred_ele...  7.02 us
    ppermute x6, waiting for transfers between devices, padded_2(): lax.ppermute(tail, axis, [(i, (i + 1) % count) for i in range(count)])  4.59 us
  transfers between devices with their start and end apart: 14, of which 5 were waited for; matrix products, arithmetic and copies ran while one was open for 5% of the time, Pallas kernels for 0%

profile of v1, /device:TPU:0, one launch (start us, length us, event | category | flops | bytes accessed | tf_op | source)
XLA Modules:
  0.0 222.7 jit_solution(5579466478931813520)
XLA Ops:
  7.2 1.3 copy.30
  8.6 0.5 collective-permute-start
  9.1 2.9 %collective-permute-start.1 = (bf16[1,32,128]{2,0,1:T(2,128)(2,1)S(1)}, bf16[1,32,128]{2,0,1:T(2,128)(2,1)S(1)}, u32[]{:S(2)}, u32[]{:S(2)}) collective-permute-start(bf16[1,32,128]{2,0,1:T(2,128)(2,1)S(1)} %get-tuple-element.41), channel_id=1, source_target_pairs={{4,0},{8,4},{12,8},{16,12},{20,16},{24,20},{28,24},{0,28},{5,1},{9... | collective-permute-start | bytes 24584 | tf_op jit(solution)/shard_map/ppermute | solution.py:17
  12.1 0.7 fusion.119
  12.8 2.6 %collective-permute-start.4 = (bf16[1,32,128]{2,1,0:T(8,128)(2,1)S(1)}, bf16[1,32,128]{2,1,0:T(8,128)(2,1)S(1)}, u32[]{:S(2)}, u32[]{:S(2)}) collective-permute-start(bf16[1,32,128]{2,1,0:T(8,128)(2,1)S(1)} %get-tuple-element.34), channel_id=1, source_target_pairs={{4,0},{8,4},{12,8},{16,12},{20,16},{24,20},{28,24},{0,28},{5,1},{9... | collective-permute-start | bytes 24584 | tf_op jit(solution)/shard_map/ppermute | solution.py:17
  15.5 2.3 %collective-permute-start.2 = (bf16[66,1,128]{2,0,1:T(8,128)(2,1)S(1)}, bf16[66,1,128]{2,0,1:T(8,128)(2,1)S(1)}, u32[]{:S(2)}, u32[]{:S(2)}) collective-permute-start(bf16[66,1,128]{2,0,1:T(8,128)(2,1)S(1)} %get-tuple-element.25), channel_id=1, source_target_pairs={{0,1},{1,2},{2,3},{3,0},{4,5},{5,6},{6,7},{7,4},{8,9},{9,10},{10,1... | collective-permute-start | bytes 50696 | tf_op jit(solution)/shard_map/ppermute | solution.py:15
  17.8 2.1 collective-permute-start.7
  20.9 0.4 pad_maximum_fusion.7
  21.3 0.3 copy.35
  21.6 0.3 copy.41
  22.0 2.0 collective-permute-start.5
  23.9 0.5 collective-permute-start.6
  24.5 0.4 pad_maximum_fusion.1
  24.8 0.7 fusion.116
  25.6 0.3 copy.33
  26.2 0.3 copy.36
  26.5 0.3 copy.37
  27.9 2.2 collective-permute-done.6
  30.1 0.7 pad_maximum_fusion.11
  32.0 0.7 copy-done.4
  35.7 0.4 fusion.21
  36.1 1.4 fusion.43
  37.9 0.4 fusion.40
  38.9 0.4 fusion.37
  40.1 2.6 %collective-permute-start.9 = (bf16[1,32,128]{2,0,1:T(2,128)(2,1)S(1)}, bf16[1,32,128]{2,0,1:T(2,128)(2,1)S(1)}, u32[]{:S(2)}, u32[]{:S(2)}) collective-permute-start(bf16[1,32,128]{2,0,1:T(2,128)(2,1)S(1)} %get-tuple-element.37), channel_id=1, source_target_pairs={{4,0},{8,4},{12,8},{16,12},{20,16},{24,20},{28,24},{0,28},{5,1},{9... | collective-permute-start | bytes 24584 | tf_op jit(solution)/shard_map/ppermute | solution.py:17
  42.7 0.3 fusion.34
  43.1 1.2 collective-permute-done.8
  44.4 4.0 %collective-permute-start.11 = (bf16[66,1,128]{2,0,1:T(8,128)(2,1)S(1)}, bf16[66,1,128]{2,0,1:T(8,128)(2,1)S(1)}, u32[]{:S(2)}, u32[]{:S(2)}) collective-permute-start(bf16[66,1,128]{2,0,1:T(8,128)(2,1)S(1)} %get-tuple-element.20), channel_id=1, source_target_pairs={{1,0},{2,1},{3,2},{0,3},{5,4},{6,5},{7,6},{4,7},{9,8},{10,9},{11,1... | collective-permute-start | bytes 50696 | tf_op jit(solution)/shard_map/ppermute | solution.py:17
  48.7 1.2 collective-permute-done.10
  49.9 0.4 pad_maximum_fusion.2
  50.3 0.4 fusion.32
  50.7 0.5 fusion.31
  51.1 0.4 fusion.30
  51.5 0.5 fusion.29
  52.0 0.4 fusion.28
  52.4 0.4 fusion.27
  52.8 0.4 fusion.26
  53.3 0.5 fusion.25
  53.7 0.4 fusion.24
  54.2 1.9 pad_maximum_fusion
  56.2 56.7 %all-reduce.3.cloned.1.call-done = f32[2,147456]{1,0:T(2,128)} async-done(((f32[2,147456]{1,0:T(2,128)}), f32[2,147456]{1,0:T(2,128)}) %all-reduce.3.cloned.1.call-update) | async-done | bytes 1179664 | tf_op jit(solution)/shard_map/psum | solution.py:108
  113.0 5.1 %copy.91 = f32[1,2,1152,128]{3,1,2,0:T(2,128)} copy(f32[1,2,1152,128]{3,2,1,0:T(8,128)S(1)} %bitcast.218) | data formatting | bytes 2359296
  118.1 54.6 %all-reduce.5.cloned.1.call-done = f32[2,147456]{1,0:T(2,128)} async-done(((f32[2,147456]{1,0:T(2,128)}), f32[2,147456]{1,0:T(2,128)}) %all-reduce.5.cloned.1.call-update) | async-done | bytes 1179664 | tf_op jit(solution)/shard_map/psum | solution.py:108
  172.7 2.5 %multiply_reduce_fusion = f32[2]{0:T(128)S(1)} fusion(f32[2,147456]{1,0:T(2,128)} %all-reduce.5.cloned.1.call-done), kind=kLoop, calls=%fused_computation.45 | loop fusion | flops 589822 | bytes 1179656 | tf_op jit(solution)/shard_map/reduce_sum | solution.py:109
  175.3 1.4 multiply_add_fusion
  176.7 33.7 %fusion = f32[2,2,147456]{2,0,1:T(2,128)S(1)} fusion(f32[32]{0:T(128)S(1)} %copy-done.9, f32[2,147456]{1,0:T(2,128)S(1)} %bitcast.239, f32[32]{0:T(128)S(1)} %get-tuple-element.43, f32[2,147456]{1,0:T(2,128)S(1)} %get-tuple-element.2, f32[32]{0:T(128)S(1)} %get-tuple-element.44, f32[2,147456]{1,0:T(2,128)S(1)} %get-tuple-element.3, ...), kind=kOutput, calls=%fused_computation.1 | convolution fusion | flops 321454080 | bytes 5899016 | tf_op jit(solution)/shard_map/kh,hlp->klp/dot_general | solution.py:83
  210.4 2.5 %fusion.23 = f32[1,2,147456]{2,0,1:T(1,128)S(1)} fusion(f32[2,2,147456]{2,0,1:T(2,128)S(1)} %fusion), kind=kLoop, calls=%fused_computation.40 | loop fusion | flops 294912 | bytes 3538944 | tf_op jit(solution)/shard_map/mul | solution.py:86
  212.9 2.7 %copy.92 = f32[1,2,147456]{2,1,0:T(2,128)} copy(f32[1,2,147456]{2,0,1:T(1,128)S(1)} %fusion.23) | data formatting | bytes 2359296
  (74 shorter events, 8.9 us)
Async XLA Ops:
  7.2 169.5 %copy-start = (f32[2,32]{1,0:T(2,128)S(1)}, f32[2,32]{1,0:T(2,128)}, u32[]{:S(2)}) copy-start(f32[2,32]{1,0:T(2,128)} %param.14) | copy-start | bytes 772
  7.2 12.7 %copy-start.3 = (bf16[64,32,128]{2,1,0:T(8,128)(2,1)S(1)}, bf16[64,32,128]{2,1,0:T(8,128)(2,1)}, u32[]{:S(2)}) copy-start(bf16[64,32,128]{2,1,0:T(8,128)(2,1)} %param.9) | copy-start | bytes 1572868
  7.2 105.7 %all-reduce.3.cloned.1.call-start = ((), (), s32[]{:S(2)}) async-start(), calls=%async_computation | async-start | bytes 2359296 | tf_op jit(solution)/shard_map/psum | solution.py:108
  8.6 6.8 %collective-permute-start = (bf16[1,32,128]{2,0,1:T(2,128)(2,1)S(1)}, bf16[1,32,128]{2,0,1:T(2,128)(2,1)S(1)}, u32[]{:S(2)}, u32[]{:S(2)}) collective-permute-start(bf16[1,32,128]{2,0,1:T(2,128)(2,1)S(1)} %get-tuple-element.40), channel_id=1, source_target_pairs={{0,4},{4,8},{8,12},{12,16},{16,20},{20,24},{24,28},{28,0},{1,5},{5... | collective-permute-start | bytes 24584 | tf_op jit(solution)/shard_map/ppermute | solution.py:15
  9.1 6.3 %collective-permute-start.1 = (bf16[1,32,128]{2,0,1:T(2,128)(2,1)S(1)}, bf16[1,32,128]{2,0,1:T(2,128)(2,1)S(1)}, u32[]{:S(2)}, u32[]{:S(2)}) collective-permute-start(bf16[1,32,128]{2,0,1:T(2,128)(2,1)S(1)} %get-tuple-element.41), channel_id=1, source_target_pairs={{4,0},{8,4},{12,8},{16,12},{20,16},{24,20},{28,24},{0,28},{5,1},{9... | collective-permute-start | bytes 24584 | tf_op jit(solution)/shard_map/ppermute | solution.py:17
  12.8 7.1 %collective-permute-start.3 = (bf16[1,32,128]{2,1,0:T(8,128)(2,1)S(1)}, bf16[1,32,128]{2,1,0:T(8,128)(2,1)S(1)}, u32[]{:S(2)}, u32[]{:S(2)}) collective-permute-start(bf16[1,32,128]{2,1,0:T(8,128)(2,1)S(1)} %get-tuple-element.35), channel_id=1, source_target_pairs={{0,4},{4,8},{8,12},{12,16},{16,20},{20,24},{24,28},{28,0},{1,5},{5... | collective-permute-start | bytes 24584 | tf_op jit(solution)/shard_map/ppermute | solution.py:15
  12.8 7.1 %collective-permute-start.4 = (bf16[1,32,128]{2,1,0:T(8,128)(2,1)S(1)}, bf16[1,32,128]{2,1,0:T(8,128)(2,1)S(1)}, u32[]{:S(2)}, u32[]{:S(2)}) collective-permute-start(bf16[1,32,128]{2,1,0:T(8,128)(2,1)S(1)} %get-tuple-element.34), channel_id=1, source_target_pairs={{4,0},{8,4},{12,8},{16,12},{20,16},{24,20},{28,24},{0,28},{5,1},{9... | collective-permute-start | bytes 24584 | tf_op jit(solution)/shard_map/ppermute | solution.py:17
  15.4 4.8 %copy-start.2 = (bf16[2,9,128,128]{3,2,1,0:T(8,128)(2,1)S(1)}, bf16[2,9,128,128]{3,2,1,0:T(8,128)(2,1)}, u32[]{:S(2)}) copy-start(bf16[2,9,128,128]{3,2,1,0:T(8,128)(2,1)} %param.10) | copy-start | bytes 1769476
  15.5 9.0 %collective-permute-start.2 = (bf16[66,1,128]{2,0,1:T(8,128)(2,1)S(1)}, bf16[66,1,128]{2,0,1:T(8,128)(2,1)S(1)}, u32[]{:S(2)}, u32[]{:S(2)}) collective-permute-start(bf16[66,1,128]{2,0,1:T(8,128)(2,1)S(1)} %get-tuple-element.25), channel_id=1, source_target_pairs={{0,1},{1,2},{2,3},{3,0},{4,5},{5,6},{6,7},{7,4},{8,9},{9,10},{10,1... | collective-permute-start | bytes 50696 | tf_op jit(solution)/shard_map/ppermute | solution.py:15
  17.8 6.7 %collective-permute-start.7 = (bf16[66,1,128]{2,0,1:T(8,128)(2,1)S(1)}, bf16[66,1,128]{2,0,1:T(8,128)(2,1)S(1)}, u32[]{:S(2)}, u32[]{:S(2)}) collective-permute-start(bf16[66,1,128]{2,0,1:T(8,128)(2,1)S(1)} %get-tuple-element.24), channel_id=1, source_target_pairs={{1,0},{2,1},{3,2},{0,3},{5,4},{6,5},{7,6},{4,7},{9,8},{10,9},{11,1... | collective-permute-start | bytes 50696 | tf_op jit(solution)/shard_map/ppermute | solution.py:17
  22.0 6.0 %collective-permute-start.5 = (bf16[66,1,128]{2,1,0:T(2,128)(2,1)S(1)}, bf16[66,1,128]{2,1,0:T(2,128)(2,1)S(1)}, u32[]{:S(2)}, u32[]{:S(2)}) collective-permute-start(bf16[66,1,128]{2,1,0:T(2,128)(2,1)S(1)} %get-tuple-element.29), channel_id=1, source_target_pairs={{1,0},{2,1},{3,2},{0,3},{5,4},{6,5},{7,6},{4,7},{9,8},{10,9},{11,1... | collective-permute-start | bytes 50696 | tf_op jit(solution)/shard_map/ppermute | solution.py:17
  23.9 6.2 %collective-permute-start.6 = (bf16[66,1,128]{2,1,0:T(2,128)(2,1)S(1)}, bf16[66,1,128]{2,1,0:T(2,128)(2,1)S(1)}, u32[]{:S(2)}, u32[]{:S(2)}) collective-permute-start(bf16[66,1,128]{2,1,0:T(2,128)(2,1)S(1)} %get-tuple-element.30), channel_id=1, source_target_pairs={{0,1},{1,2},{2,3},{3,0},{4,5},{5,6},{6,7},{7,4},{8,9},{9,10},{10,1... | collective-permute-start | bytes 50696 | tf_op jit(solution)/shard_map/ppermute | solution.py:15
  31.7 1.0 copy-start.4
  40.0 4.2 %collective-permute-start.8 = (bf16[1,32,128]{2,0,1:T(2,128)(2,1)S(1)}, bf16[1,32,128]{2,0,1:T(2,128)(2,1)S(1)}, u32[]{:S(2)}, u32[]{:S(2)}) collective-permute-start(bf16[1,32,128]{2,0,1:T(2,128)(2,1)S(1)} %get-tuple-element.36), channel_id=1, source_target_pairs={{0,4},{4,8},{8,12},{12,16},{16,20},{20,24},{24,28},{28,0},{1,5},{5... | collective-permute-start | bytes 24584 | tf_op jit(solution)/shard_map/ppermute | solution.py:15
  40.1 4.2 %collective-permute-start.9 = (bf16[1,32,128]{2,0,1:T(2,128)(2,1)S(1)}, bf16[1,32,128]{2,0,1:T(2,128)(2,1)S(1)}, u32[]{:S(2)}, u32[]{:S(2)}) collective-permute-start(bf16[1,32,128]{2,0,1:T(2,128)(2,1)S(1)} %get-tuple-element.37), channel_id=1, source_target_pairs={{4,0},{8,4},{12,8},{16,12},{20,16},{24,20},{28,24},{0,28},{5,1},{9... | collective-permute-start | bytes 24584 | tf_op jit(solution)/shard_map/ppermute | solution.py:17
  44.3 5.6 %collective-permute-start.10 = (bf16[66,1,128]{2,0,1:T(8,128)(2,1)S(1)}, bf16[66,1,128]{2,0,1:T(8,128)(2,1)S(1)}, u32[]{:S(2)}, u32[]{:S(2)}) collective-permute-start(bf16[66,1,128]{2,0,1:T(8,128)(2,1)S(1)} %get-tuple-element.21), channel_id=1, source_target_pairs={{0,1},{1,2},{2,3},{3,0},{4,5},{5,6},{6,7},{7,4},{8,9},{9,10},{10,1... | collective-permute-start | bytes 50696 | tf_op jit(solution)/shard_map/ppermute | solution.py:15
  44.4 5.5 %collective-permute-start.11 = (bf16[66,1,128]{2,0,1:T(8,128)(2,1)S(1)}, bf16[66,1,128]{2,0,1:T(8,128)(2,1)S(1)}, u32[]{:S(2)}, u32[]{:S(2)}) collective-permute-start(bf16[66,1,128]{2,0,1:T(8,128)(2,1)S(1)} %get-tuple-element.20), channel_id=1, source_target_pairs={{1,0},{2,1},{3,2},{0,3},{5,4},{6,5},{7,6},{4,7},{9,8},{10,9},{11,1... | collective-permute-start | bytes 50696 | tf_op jit(solution)/shard_map/ppermute | solution.py:17
  56.1 116.6 %all-reduce.5.cloned.1.call-start = ((), (), s32[]{:S(2)}) async-start(), calls=%async_computation.1 | async-start | bytes 2359296 | tf_op jit(solution)/shard_map/psum | solution.py:108
  113.0 5.1 %copy-start.8 = (f32[32,3]{0,1:T(4,128)S(1)}, f32[32,3]{0,1:T(4,128)}, u32[]{:S(2)}) copy-start(f32[32,3]{0,1:T(4,128)} %param.12) | copy-start | bytes 1156
  113.0 62.2 %copy-start.5 = (f32[2,147456]{1,0:T(2,128)S(1)}, f32[2,147456]{1,0:T(2,128)}, u32[]{:S(2)}) copy-start(f32[2,147456]{1,0:T(2,128)} %param.11) | copy-start | bytes 3538948
  172.7 2.5 %copy-start.1 = (f32[2,147456]{1,0:T(2,128)S(1)}, f32[2,147456]{1,0:T(2,128)}, u32[]{:S(2)}) copy-start(f32[2,147456]{1,0:T(2,128)} %all-reduce.5.cloned.1.call-done) | copy-start | bytes 3538948
  175.2 1.4 copy-start.7
  175.2 1.4 copy-start.9
  175.2 1.4 copy-start.10
  176.6 33.8 %copy-start.6 = (f32[2,147456]{1,0:T(2,128)}, f32[2,147456]{1,0:T(2,128)S(1)}, u32[]{:S(2)}) copy-start(f32[2,147456]{1,0:T(2,128)S(1)} %get-tuple-element.2) | copy-start | bytes 3538948
Sparse Core Ops, SparseCore 0:
  56.2 56.5 all-reduce.2
  116.0 56.6 all-reduce.4
